TPU v7x, 32 devices: a whole 2x2x4 slice. The times are simulated.
32 devices in a mesh: ep: 8 (over z, y), tp: 4 (over x, core).
Axes of the slice: x: 2, y: 2, z: 4, core: 2. Of those that a mesh axis runs over, the one named last changes fastest.
Arguments:
- tokens: bfloat16 [1024, 3584], P('ep', 'tp'), may hold values from -6 to 6
- tangents: bfloat16 [2, 1024, 3584], P(None, 'ep', 'tp'), may hold values from -6 to 6
- tangent_mask: int32 [2, 1024, 28], P(None, 'ep', 'tp'), may hold values 0 or 1
- expert_ids: int32 [1024, 2], P('ep'), may hold values from 0 to 7, all different within a row; in each aligned block of 128 rows (0 to 127, 128 to 255, ...) at most 48 rows name the same one
- gate_fixed: int32 [1024, 2], P('ep'), may hold values from 4096 to 65535
- w_up: bfloat16 [8, 3584, 1024], P('ep', None, 'tp'), may hold values from -0.09375 to 0.09375
- w_down: bfloat16 [8, 1024, 3584], P('ep', None, 'tp'), may hold values from -0.1875 to 0.1875
Outputs:
- mixed: bfloat16 [1024, 3584], P('ep', 'tp')
- mixed_tangents: bfloat16 [2, 1024, 3584], P(None, 'ep', 'tp')
Inputs may be any that keep to these rules, and one draw needn't show every extreme that they name: `expert_ids`: each row names 2 different experts; among the rows of the tokens of one index of ep (128 aligned rows) no expert is named by more than 48 rows, a bound that some block reaches.
All inputs are finite; a program needn't handle non-finite values. No bound on the sum of `tangent_mask` on one device may be relied on, other than what follows from the above.
Results may differ from a plain program's by a relative error of at most 0.008.
Values may be sent and summed in bfloat16 or wider, within the bound.
A program may use at most 64 MiB of HBM per device.

v0:
```python
import jax
import jax.numpy as jnp
from jax import lax
from jax.sharding import PartitionSpec as P


def body(tokens, tangents, tangent_mask, expert_ids, gate_fixed, w_up, w_down):
    group, quarter = tokens.shape
    n_ep = lax.axis_size("ep")
    top = expert_ids.shape[1]
    local_experts = w_up.shape[0]
    experts = local_experts * n_ep
    capacity = max(2, min(group, 3 * group * top // (2 * experts)))
    blocks = tangent_mask.shape[2]
    keep = tangent_mask.astype(jnp.bfloat16)
    masked = (tangents.reshape(2, group, blocks, quarter // blocks) * keep[..., None]).reshape(
        2, group, quarter
    )
    stacked = jnp.concatenate([tokens[None], masked], axis=0)
    flat_ids = expert_ids.reshape(-1)
    onehot = (flat_ids[:, None] == jnp.arange(experts, dtype=jnp.int32)[None, :]).astype(jnp.int32)
    rank = jnp.sum((jnp.cumsum(onehot, axis=0) - onehot) * onehot, axis=1)
    dest = flat_ids * capacity + rank
    owner = jnp.full((experts * capacity,), group, jnp.int32)
    owner = owner.at[dest].set(jnp.arange(group * top, dtype=jnp.int32) // top)
    send_cols = jnp.take(stacked, owner, axis=1, mode="fill", fill_value=0)
    send_cols = send_cols.reshape(3, n_ep, local_experts * capacity, quarter)
    arrived = lax.all_to_all(send_cols, "ep", split_axis=1, concat_axis=1, tiled=True)
    routed = arrived.reshape(3, n_ep, local_experts, capacity, quarter)
    weights = w_up
    hidden = jnp.einsum(
        "tsecd,edf->tsecf",
        lax.all_gather(routed, "tp", axis=4, tiled=True),
        weights,
        preferred_element_type=jnp.float32,
    )
    base = hidden[0]
    sig = jax.nn.sigmoid(base)
    slope = sig * (1.0 + base * (1.0 - sig))
    acts = jnp.concatenate([(base * sig)[None], slope[None] * hidden[1:]], axis=0).astype(
        jnp.bfloat16
    )
    out_width = w_down.shape[2]
    weights = w_down
    outs = jnp.einsum(
        "tsecf,efd->tsecd",
        lax.all_gather(acts, "tp", axis=4, tiled=True),
        weights,
        preferred_element_type=jnp.float32,
    ).astype(jnp.bfloat16)
    outs = outs.reshape(3, n_ep, local_experts * capacity, out_width)
    returned = lax.all_to_all(outs, "ep", split_axis=1, concat_axis=1, tiled=True)
    table = returned.reshape(3, experts * capacity, out_width)
    picked = jnp.take(table, dest, axis=1).reshape(3, group, top, out_width)
    gates = gate_fixed.astype(jnp.float32) / 65536.0
    summed = jnp.einsum("tgkd,gk->tgd", picked.astype(jnp.float32), gates).astype(jnp.bfloat16)
    return (summed[0], summed[1:])


def solution(mesh):
    placed = (
        P("ep", "tp"),
        P(None, "ep", "tp"),
        P(None, "ep", "tp"),
        P("ep", None),
        P("ep", None),
        P("ep", None, "tp"),
        P("ep", None, "tp"),
    )
    return jax.shard_map(
        body,
        mesh=mesh,
        in_specs=placed,
        out_specs=(P("ep", "tp"), P(None, "ep", "tp")),
        check_vma=False,
    )
```

profile of v0, /device:TPU:0, one launch (start us, length us, event | category | flops | bytes accessed | tf_op | source)
XLA Modules:
  0.0 249.6 jit_solution(13066110364712202970)
XLA Ops:
  7.2 0.0 copy-start
  7.2 0.0 copy-start.1
  7.2 0.0 all-gather.6.cloned.1.call-start
  7.2 1.0 copy.39
  8.2 0.1 eq.26
  8.3 0.1 reshape.144
  8.5 0.7 broadcast_multiply_fusion
  9.2 0.6 reduce-window.6
  9.8 0.2 slice_reduce_fusion
  10.0 0.1 copy.43
  10.1 0.1 mul.64
  10.3 0.1 fusion.16
  10.4 1.4 scatter_custom_fusion
  11.8 0.7 convert_element_type.38
  12.5 0.1 mul.65
  12.6 0.7 copy.46
  13.3 0.0 copy-done.1
  13.3 0.4 copy.47
  13.7 0.1 broadcast_in_dim.37
  13.8 1.6 copy_multiply_fusion
  15.4 0.9 pad_maximum_fusion
  16.4 5.0 %gather_fusion = bf16[384,3,896]{2,1,0:T(4,128)(2,1)} fusion(bf16[3,128,896]{2,0,1:T(4,128)(2,1)S(1)} %pad_maximum_fusion, s32[1024]{0:T(1024)S(1)} %pad_clamp_fusion.1), kind=kCustom, calls=%fused_computation | custom fusion | bytes 4130304 | tf_op jit(solution)/shard_map/jit(_take)/gather | solution.py:26
  21.4 2.2 copy_select_fusion
  23.6 54.6 %all_to_all.10 = bf16[3,8,48,896]{3,2,0,1:T(8,128)(2,1)S(1)} all-to-all(bf16[3,8,48,896]{3,2,0,1:T(8,128)(2,1)S(1)} %copy_select_fusion), channel_id=1, replica_groups=mesh['ep'=8,'tp'=4] {'ep'}, dimensions={1} | all-to-all | bytes 4128768 | tf_op jit(solution)/shard_map/all_to_all | solution.py:28
  78.2 1.6 copy.49
  79.8 0.0 all-gather.6.cloned.1.call-update
  79.8 0.0 all-gather.4.cloned.1.call-start
  79.9 56.6 %all-gather.6.cloned.1.call-done = bf16[3,8,48,3584]{3,2,1,0:T(8,128)(2,1)} async-done(((bf16[3,8,48,896]{3,2,1,0:T(8,128)(2,1)}), bf16[3,8,48,3584]{3,2,1,0:T(8,128)(2,1)}) %all-gather.6.cloned.1.call-update) | async-done | bytes 8257552 | tf_op jit(solution)/shard_map/all_gather | solution.py:33
  136.5 6.2 %fusion.8 = f32[3,8,1,48,256]{4,3,1,0,2:T(8,128)S(1)} fusion(bf16[3,8,48,3584]{3,2,1,0:T(8,128)(2,1)} %all-gather.6.cloned.1.call-done, bf16[1,3584,256]{2,1,0:T(8,128)(2,1)} %param.12), kind=kOutput, calls=%fused_computation.11 | convolution fusion | flops 2113929216 | bytes 11272192 | tf_op jit(solution)/shard_map/tsecd,edf->tsecf/dot_general | solution.py:31
  142.6 0.2 multiply_convert_fusion
  142.8 0.1 fusion.13
  142.9 0.9 pad_maximum_fusion.1
  143.8 0.0 all-gather.4.cloned.1.call-update
  143.8 24.5 %all-gather.4.cloned.1.call-done = bf16[3,8,1,48,1024]{4,3,1,0,2:T(8,128)(2,1)} async-done(((bf16[3,8,1,48,256]{4,3,1,0,2:T(8,128)(2,1)}), bf16[3,8,1,48,1024]{4,3,1,0,2:T(8,128)(2,1)}) %all-gather.4.cloned.1.call-update) | async-done | bytes 2359312 | tf_op jit(solution)/shard_map/all_gather | solution.py:47
  168.3 0.0 copy-done
  168.3 4.3 %fusion.2 = bf16[3,8,48,896]{3,2,1,0:T(8,128)(2,1)S(1)} fusion(bf16[3,8,1,48,1024]{4,3,1,0,2:T(8,128)(2,1)} %all-gather.4.cloned.1.call-done, bf16[1,1024,896]{2,1,0:T(8,128)(2,1)S(1)} %copy-done), kind=kOutput, calls=%fused_computation.6 | convolution fusion | flops 2114961408 | bytes 6258688 | tf_op jit(solution)/shard_map/tsecf,efd->tsecd/dot_general | solution.py:45
  172.6 1.5 copy.50
  174.1 0.0 copy-start.2
  174.1 0.0 copy-start.3
  174.1 5.6 %all-to-all-start.1 = ((bf16[3,8,48,896]{3,2,0,1:T(8,128)(2,1)}), bf16[3,8,48,896]{3,2,0,1:T(8,128)(2,1)}, u32[]{:S(2)}, u32[]{:S(2)}) async-start(bf16[3,8,48,896]{3,2,0,1:T(8,128)(2,1)} %copy.50), calls=%async_computation.1 | async-start | bytes 4128768 | tf_op jit(solution)/shard_map/all_to_all | solution.py:52
  179.7 0.1 reduce_sum.14
  179.9 0.1 copy.41
  179.9 0.0 copy-done.2
  180.0 0.1 copy.42
  180.1 0.0 copy-done.3
  180.1 0.1 copy.54
  180.3 47.5 %all-to-all-done.1 = bf16[3,8,48,896]{3,2,0,1:T(8,128)(2,1)} async-done(((bf16[3,8,48,896]{3,2,0,1:T(8,128)(2,1)}), bf16[3,8,48,896]{3,2,0,1:T(8,128)(2,1)}, u32[]{:S(2)}, u32[]{:S(2)}) %all-to-all-start.1) | async-done | bytes 2064416 | tf_op jit(solution)/shard_map/all_to_all | solution.py:52
  227.8 4.3 %copy.51 = bf16[3,8,48,896]{3,0,2,1:T(4,128)(2,1)} copy(bf16[3,8,48,896]{3,2,0,1:T(8,128)(2,1)} %all-to-all-done.1) | data formatting | bytes 4128768 | tf_op jit(solution)/shard_map/all_to_all | solution.py:52
  232.1 5.2 %gather_fusion.1 = bf16[256,3,896]{2,1,0:T(4,128)(2,1)} fusion(bf16[3,384,896]{2,0,1:T(4,128)(2,1)} %bitcast.63, s32[1024]{0:T(1024)S(1)} %pad_clamp_fusion), kind=kCustom, calls=%fused_computation.1 | custom fusion | bytes 2753536 | tf_op jit(solution)/shard_map/jit(_take)/gather | solution.py:54
  237.2 2.3 broadcast_select_fusion
  239.5 1.6 fusion.11
  241.2 0.1 copy.64
  241.2 0.8 slice.32
  242.1 0.7 slice_bitcast_fusion
  (12 shorter events, 0.1 us)
Async XLA Ops:
  7.2 161.1 %copy-start = (bf16[1,1024,896]{2,1,0:T(8,128)(2,1)S(1)}, bf16[1,1024,896]{2,1,0:T(8,128)(2,1)}, u32[]{:S(2)}) copy-start(bf16[1,1024,896]{2,1,0:T(8,128)(2,1)} %param.13) | copy-start | bytes 5505028
  7.2 6.2 %copy-start.1 = (bf16[128,896]{1,0:T(8,128)(2,1)S(1)}, bf16[128,896]{1,0:T(8,128)(2,1)}, u32[]{:S(2)}) copy-start(bf16[128,896]{1,0:T(8,128)(2,1)} %param.7) | copy-start | bytes 688132
  7.2 129.3 %all-gather.6.cloned.1.call-start = ((), (), s32[]{:S(2)}) async-start(), calls=%async_computation.3 | async-start | bytes 10321920 | tf_op jit(solution)/shard_map/all_gather | solution.py:33
  79.8 88.5 %all-gather.4.cloned.1.call-start = ((), (), s32[]{:S(2)}) async-start(), calls=%async_computation.2 | async-start | bytes 2949120 | tf_op jit(solution)/shard_map/all_gather | solution.py:47
  174.1 5.9 %copy-start.2 = (s32[128,2]{0,1:T(2,128)S(1)}, s32[128,2]{0,1:T(2,128)}, u32[]{:S(2)}) copy-start(s32[128,2]{0,1:T(2,128)} %param.10) | copy-start | bytes 3076
  174.1 6.0 %copy-start.3 = (s32[128,2]{0,1:T(2,128)S(1)}, s32[128,2]{0,1:T(2,128)}, u32[]{:S(2)}) copy-start(s32[128,2]{0,1:T(2,128)} %param.11) | copy-start | bytes 3076
  174.1 53.7 %all-to-all-start.1 = ((bf16[3,8,48,896]{3,2,0,1:T(8,128)(2,1)}), bf16[3,8,48,896]{3,2,0,1:T(8,128)(2,1)}, u32[]{:S(2)}, u32[]{:S(2)}) async-start(bf16[3,8,48,896]{3,2,0,1:T(8,128)(2,1)} %copy.50), calls=%async_computation.1 | async-start | bytes 4128768 | tf_op jit(solution)/shard_map/all_to_all | solution.py:52
Sparse Core Ops, SparseCore 0:
  79.9 56.4 all-gather.5
  143.9 24.3 all-gather.3
where the time goes:
time: 250 us
  waiting for transfers between devices  129 us (52%)
  blocking collectives  54.6 us (22%)
  local copies, waits for them, and re-layouts  24 us (10%)
  between operations  14.2 us (6%)
  matrix products  12.1 us (5%)
  other arithmetic  10.3 us (4%)
  starting transfers between devices  5.73 us (2%)
    all_gather x1, waiting for transfers between devices, body(): lax.all_gather(routed, 'tp', axis=4, tiled=True)  56.6 us
    all_to_all x1, blocking collectives, body(): lax.all_to_all(send_cols, 'ep', split_axis=1, concat_axis=1, tiled=True)  54.6 us
    all_to_all x1, waiting for transfers between devices, body(): lax.all_to_all(outs, 'ep', split_axis=1, concat_axis=1, tiled=True)  47.5 us
    all_gather x1, waiting for transfers between devices, body(): lax.all_gather(acts, 'tp', axis=4, tiled=True)  24.5 us
    dot_general x1, matrix products, body(): jnp.einsum('tsecd,edf->tsecf', lax.all_gather(routed, 'tp', axis=4, tiled...  6.16 us
    all_to_all x1, starting transfers between devices, body(): lax.all_to_all(outs, 'ep', split_axis=1, concat_axis=1, tiled=True)  5.65 us
    gather x1, local copies, waits for them, and re-layouts, body(): picked = jnp.take(table, dest, axis=1).reshape(3, group, top, out_width)  5.17 us
    gather x1, local copies, waits for them, and re-layouts, body(): send_cols = jnp.take(stacked, owner, axis=1, mode='fill', fill_value=0)  5.02 us
  transfers between devices with their start and end apart: 3, of which 3 were waited for; matrix products, arithmetic and copies ran while one was open for 0% of the time, Pallas kernels for 0%

commit v1 on v0

--- a/solution.py
+++ b/solution.py
@@ -2,6 +2,17 @@
 import jax.numpy as jnp
 from jax import lax
 from jax.sharding import PartitionSpec as P
+
+
+def collect(array, axis, dim):
+    ways = lax.axis_size(axis)
+    pieces = [array]
+    for far in range(1, ways):
+        pieces.append(
+            lax.ppermute(pieces[far - 1], axis, [(d, (d - 1) % ways) for d in range(ways)])
+        )
+    line = jnp.concatenate(pieces, axis=dim)
+    return jnp.roll(line, lax.axis_index(axis) * array.shape[dim], axis=dim)
 
 
 def body(tokens, tangents, tangent_mask, expert_ids, gate_fixed, w_up, w_down):
@@ -43,10 +54,7 @@
     out_width = w_down.shape[2]
     weights = w_down
     outs = jnp.einsum(
-        "tsecf,efd->tsecd",
-        lax.all_gather(acts, "tp", axis=4, tiled=True),
-        weights,
-        preferred_element_type=jnp.float32,
+        "tsecf,efd->tsecd", collect(acts, "tp", 4), weights, preferred_element_type=jnp.float32
     ).astype(jnp.bfloat16)
     outs = outs.reshape(3, n_ep, local_experts * capacity, out_width)
     returned = lax.all_to_all(outs, "ep", split_axis=1, concat_axis=1, tiled=True)

time: 250 us -> 261 us (1.044)
  local copies, waits for them, and re-layouts: 24 us -> 32.4 us
  starting transfers between devices: 5.73 us -> 9.91 us
  waiting for transfers between devices: 129 us -> 125 us
    all_gather x1 -> x0, waiting for transfers between devices: 24.5 us -> none  [body(): lax.all_gather(acts, 'tp', axis=4, tiled=True)]
    ppermute x0 -> x3, waiting for transfers between devices: none -> 20.4 us  [collect(): lax.ppermute(pieces[far - 1], axis, [(d, (d - 1) % ways) for d in range(w...]
    unnamed x9 -> x16, local copies, waits for them, and re-layouts: 0.99 us -> 6.5 us
    ppermute x0 -> x3, starting transfers between devices: none -> 4.02 us  [collect(): lax.ppermute(pieces[far - 1], axis, [(d, (d - 1) % ways) for d in range(w...]
  transfers between devices with their start and end apart: 3 -> 5, of which waited for: 3 -> 5; matrix products, arithmetic and copies ran while one was open for 0% -> 1% of each run, Pallas kernels for 0% -> 0%
where the time goes in v1:
time: 261 us; the launch traced here: 260 us
  waiting for transfers between devices  125 us (48%)
  blocking collectives  54.6 us (21%)
  local copies, waits for them, and re-layouts  32.4 us (12%)
  between operations  14.2 us (5%)
  matrix products  12.1 us (5%)
  other arithmetic  11.4 us (4%)
  starting transfers between devices  9.91 us (4%)
    all_gather x1, waiting for transfers between devices, body(): lax.all_gather(routed, 'tp', axis=4, tiled=True)  56.6 us
    all_to_all x1, blocking collectives, body(): lax.all_to_all(send_cols, 'ep', split_axis=1, concat_axis=1, tiled=True)  54.6 us
    all_to_all x1, waiting for transfers between devices, body(): lax.all_to_all(outs, 'ep', split_axis=1, concat_axis=1, tiled=True)  48.3 us
    ppermute x3, waiting for transfers between devices, collect(): lax.ppermute(pieces[far - 1], axis, [(d, (d - 1) % ways) for d in range(w...  20.4 us
    unnamed x16, local copies, waits for them, and re-layouts  6.5 us
    dot_general x1, matrix products, body(): jnp.einsum('tsecd,edf->tsecf', lax.all_gather(routed, 'tp', axis=4, tiled...  6.16 us
    all_to_all x1, starting transfers between devices, body(): lax.all_to_all(outs, 'ep', split_axis=1, concat_axis=1, tiled=True)  5.86 us
  transfers between devices with their start and end apart: 5, of which 5 were waited for; matrix products, arithmetic and copies ran while one was open for 1% of the time, Pallas kernels for 0%

profile of v1, /device:TPU:0, one launch (start us, length us, event | category | flops | bytes accessed | tf_op | source)
XLA Modules:
  0.0 259.9 jit_solution(14551567585996277777)
XLA Ops:
  7.2 0.0 copy-start
  7.2 0.0 all-gather.3.cloned.1.call-start
  7.2 0.9 copy.39
  8.1 0.1 eq.29
  8.3 0.1 reshape.144
  8.4 0.7 broadcast_multiply_fusion
  9.1 0.6 reduce-window.6
  9.7 0.2 slice_reduce_fusion
  9.9 0.1 copy.43
  10.1 0.1 mul.67
  10.2 0.1 fusion.17
  10.3 1.4 scatter_custom_fusion
  11.8 0.7 convert_element_type.38
  12.5 0.1 mul.68
  12.5 0.7 copy.46
  13.3 1.3 copy.47
  14.6 0.1 broadcast_in_dim.37
  14.7 1.6 copy_multiply_fusion
  16.3 0.9 pad_maximum_fusion
  17.2 5.0 %gather_fusion = bf16[384,3,896]{2,1,0:T(4,128)(2,1)} fusion(bf16[3,128,896]{2,0,1:T(4,128)(2,1)S(1)} %pad_maximum_fusion, s32[1024]{0:T(1024)S(1)} %pad_clamp_fusion.1), kind=kCustom, calls=%fused_computation | custom fusion | bytes 4130304 | tf_op jit(solution)/shard_map/jit(_take)/gather | solution.py:37
  22.3 2.2 copy_select_fusion
  24.5 54.6 %all_to_all.10 = bf16[3,8,48,896]{3,2,0,1:T(8,128)(2,1)S(1)} all-to-all(bf16[3,8,48,896]{3,2,0,1:T(8,128)(2,1)S(1)} %copy_select_fusion), channel_id=1, replica_groups=mesh['ep'=8,'tp'=4] {'ep'}, dimensions={1} | all-to-all | bytes 4128768 | tf_op jit(solution)/shard_map/all_to_all | solution.py:39
  79.1 1.6 copy.49
  80.6 0.0 all-gather.3.cloned.1.call-update
  80.7 56.6 %all-gather.3.cloned.1.call-done = bf16[3,8,48,3584]{3,2,1,0:T(8,128)(2,1)} async-done(((bf16[3,8,48,896]{3,2,1,0:T(8,128)(2,1)}), bf16[3,8,48,3584]{3,2,1,0:T(8,128)(2,1)}) %all-gather.3.cloned.1.call-update) | async-done | bytes 8257552 | tf_op jit(solution)/shard_map/all_gather | solution.py:44
  137.3 6.2 %fusion.9 = f32[3,8,1,48,256]{4,3,1,0,2:T(8,128)S(1)} fusion(bf16[3,8,48,3584]{3,2,1,0:T(8,128)(2,1)} %all-gather.3.cloned.1.call-done, bf16[1,3584,256]{2,1,0:T(8,128)(2,1)} %param.12), kind=kOutput, calls=%fused_computation.12 | convolution fusion | flops 2113929216 | bytes 11272192 | tf_op jit(solution)/shard_map/tsecd,edf->tsecf/dot_general | solution.py:42
  143.5 0.2 multiply_convert_fusion
  143.6 0.0 copy-start.1
  143.6 0.1 fusion.14
  143.8 1.0 pad_maximum_fusion.1
  144.8 0.2 collective-permute-start
  145.0 7.4 %collective-permute-done = bf16[3,8,1,48,256]{4,3,1,0,2:T(8,128)(2,1)S(1)} collective-permute-done((bf16[3,8,1,48,256]{4,3,1,0,2:T(8,128)(2,1)S(1)}, bf16[3,8,1,48,256]{4,3,1,0,2:T(8,128)(2,1)S(1)}, u32[]{:S(2)}, u32[]{:S(2)}) %collective-permute-start) | collective-permute-done | bytes 589856 | tf_op jit(solution)/shard_map/ppermute | solution.py:12
  152.4 1.9 collective-permute-start.1
  154.3 7.4 %collective-permute-done.1 = bf16[3,8,1,48,256]{4,3,1,0,2:T(8,128)(2,1)S(1)} collective-permute-done((bf16[3,8,1,48,256]{4,3,1,0,2:T(8,128)(2,1)S(1)}, bf16[3,8,1,48,256]{4,3,1,0,2:T(8,128)(2,1)S(1)}, u32[]{:S(2)}, u32[]{:S(2)}) %collective-permute-start.1) | collective-permute-done | bytes 589856 | tf_op jit(solution)/shard_map/ppermute | solution.py:12
  161.7 0.0 copy-done.1
  161.7 1.9 collective-permute-start.2
  163.6 0.0 copy-start.2
  163.6 0.9 constant_dynamic-update-slice_fusion.6
  164.5 0.9 constant_dynamic-update-slice_fusion.5
  165.4 5.6 %collective-permute-done.2 = bf16[3,8,1,48,256]{4,3,1,0,2:T(8,128)(2,1)} collective-permute-done((bf16[3,8,1,48,256]{4,3,1,0,2:T(8,128)(2,1)S(1)}, bf16[3,8,1,48,256]{4,3,1,0,2:T(8,128)(2,1)}, u32[]{:S(2)}, u32[]{:S(2)}) %collective-permute-start.2) | collective-permute-done | bytes 589856 | tf_op jit(solution)/shard_map/ppermute | solution.py:12
  171.0 2.0 constant_dynamic-update-slice_fusion.4
  173.0 0.0 copy-done.2
  173.0 0.9 constant_dynamic-update-slice_fusion.3
  173.8 0.9 constant_dynamic-update-slice_fusion.2
  174.7 0.9 constant_dynamic-update-slice_fusion.1
  175.6 2.0 constant_dynamic-update-slice_fusion
  177.6 0.0 copy-done
  177.6 4.3 %fusion.3 = bf16[3,8,48,896]{3,2,1,0:T(8,128)(2,1)S(1)} fusion(bf16[3,8,1,48,2048]{4,3,1,0,2:T(8,128)(2,1)} %constant_dynamic-update-slice_fusion, s32[]{:T(128)S(6)} %select_n.56, bf16[1,1024,896]{2,1,0:T(8,128)(2,1)S(1)} %copy-done), kind=kOutput, calls=%fused_computation.7 | convolution fusion | flops 2114961408 | bytes 6258692 | tf_op jit(solution)/shard_map/tsecf,efd->tsecd/dot_general | solution.py:56
  181.9 1.5 copy.50
  183.4 5.9 %all-to-all-start.1 = ((bf16[3,8,48,896]{3,2,0,1:T(8,128)(2,1)}), bf16[3,8,48,896]{3,2,0,1:T(8,128)(2,1)}, u32[]{:S(2)}, u32[]{:S(2)}) async-start(bf16[3,8,48,896]{3,2,0,1:T(8,128)(2,1)} %copy.50), calls=%async_computation.1 | async-start | bytes 4128768 | tf_op jit(solution)/shard_map/all_to_all | solution.py:60
  189.2 0.1 reduce_sum.14
  189.4 0.1 copy.41
  189.4 0.0 copy-done.3
  189.5 0.1 copy.42
  189.6 0.0 copy-done.4
  189.6 0.1 copy.54
  189.8 48.3 %all-to-all-done.1 = bf16[3,8,48,896]{3,2,0,1:T(8,128)(2,1)} async-done(((bf16[3,8,48,896]{3,2,0,1:T(8,128)(2,1)}), bf16[3,8,48,896]{3,2,0,1:T(8,128)(2,1)}, u32[]{:S(2)}, u32[]{:S(2)}) %all-to-all-start.1) | async-done | bytes 2064416 | tf_op jit(solution)/shard_map/all_to_all | solution.py:60
  238.1 4.3 %copy.51 = bf16[3,8,48,896]{3,0,2,1:T(4,128)(2,1)} copy(bf16[3,8,48,896]{3,2,0,1:T(8,128)(2,1)} %all-to-all-done.1) | data formatting | bytes 4128768 | tf_op jit(solution)/shard_map/all_to_all | solution.py:60
  242.4 5.2 %gather_fusion.1 = bf16[256,3,896]{2,1,0:T(4,128)(2,1)} fusion(bf16[3,384,896]{2,0,1:T(4,128)(2,1)} %bitcast.63, s32[1024]{0:T(1024)S(1)} %pad_clamp_fusion), kind=kCustom, calls=%fused_computation.1 | custom fusion | bytes 2753536 | tf_op jit(solution)/shard_map/jit(_take)/gather | solution.py:62
  247.6 2.3 broadcast_select_fusion
  249.8 1.6 fusion.12
  251.5 0.1 copy.64
  251.6 0.8 slice.32
  252.4 0.7 slice_bitcast_fusion
  (14 shorter events, 0.1 us)
Async XLA Ops:
  7.2 170.4 %copy-start = (bf16[1,1024,896]{2,1,0:T(8,128)(2,1)S(1)}, bf16[1,1024,896]{2,1,0:T(8,128)(2,1)}, u32[]{:S(2)}) copy-start(bf16[1,1024,896]{2,1,0:T(8,128)(2,1)} %param.13) | copy-start | bytes 5505028
  7.2 130.1 %all-gather.3.cloned.1.call-start = ((), (), s32[]{:S(2)}) async-start(), calls=%async_computation.2 | async-start | bytes 10321920 | tf_op jit(solution)/shard_map/all_gather | solution.py:44
  143.6 18.0 %copy-start.1 = (bf16[1,8,1,48,256]{4,3,1,0,2:T(8,128)(2,1)}, bf16[1,8,1,48,256]{4,3,1,0,2:T(8,128)(2,1)S(1)}, u32[]{:S(2)}) copy-start(bf16[1,8,1,48,256]{4,3,1,0,2:T(8,128)(2,1)S(1)} %get-tuple-element.2) | copy-start | bytes 589828
  144.8 7.6 %collective-permute-start = (bf16[3,8,1,48,256]{4,3,1,0,2:T(8,128)(2,1)S(1)}, bf16[3,8,1,48,256]{4,3,1,0,2:T(8,128)(2,1)S(1)}, u32[]{:S(2)}, u32[]{:S(2)}) collective-permute-start(bf16[3,8,1,48,256]{4,3,1,0,2:T(8,128)(2,1)S(1)} %get-tuple-element.4), channel_id=1, source_target_pairs={{0,3},{1,0},{2,1},{3,2},{4,7},{5,4},{6,5},{7,6},{8,11},{9,8},{10,9... | collective-permute-start | bytes 1769480 | tf_op jit(solution)/shard_map/ppermute | solution.py:12
  152.4 9.3 %collective-permute-start.1 = (bf16[3,8,1,48,256]{4,3,1,0,2:T(8,128)(2,1)S(1)}, bf16[3,8,1,48,256]{4,3,1,0,2:T(8,128)(2,1)S(1)}, u32[]{:S(2)}, u32[]{:S(2)}) collective-permute-start(bf16[3,8,1,48,256]{4,3,1,0,2:T(8,128)(2,1)S(1)} %collective-permute-done), channel_id=1, source_target_pairs={{0,3},{1,0},{2,1},{3,2},{4,7},{5,4},{6,5},{7,6},{8,11},{9,8},{10,9... | collective-permute-start | bytes 1769480 | tf_op jit(solution)/shard_map/ppermute | solution.py:12
  161.7 9.3 %collective-permute-start.2 = (bf16[3,8,1,48,256]{4,3,1,0,2:T(8,128)(2,1)S(1)}, bf16[3,8,1,48,256]{4,3,1,0,2:T(8,128)(2,1)}, u32[]{:S(2)}, u32[]{:S(2)}) collective-permute-start(bf16[3,8,1,48,256]{4,3,1,0,2:T(8,128)(2,1)S(1)} %collective-permute-done.1), channel_id=1, source_target_pairs={{0,3},{1,0},{2,1},{3,2},{4,7},{5,4},{6,5},{7,6},{8,11},{9,8},{10,9... | collective-permute-start | bytes 1769480 | tf_op jit(solution)/shard_map/ppermute | solution.py:12
  163.6 9.4 %copy-start.2 = (bf16[1,8,1,48,256]{4,3,1,0,2:T(8,128)(2,1)S(1)}, bf16[1,8,1,48,256]{4,3,1,0,2:T(8,128)(2,1)}, u32[]{:S(2)}) copy-start(bf16[1,8,1,48,256]{4,3,1,0,2:T(8,128)(2,1)} %copy-done.1) | copy-start | bytes 589828
  183.4 6.1 %copy-start.3 = (s32[128,2]{0,1:T(2,128)S(1)}, s32[128,2]{0,1:T(2,128)}, u32[]{:S(2)}) copy-start(s32[128,2]{0,1:T(2,128)} %param.10) | copy-start | bytes 3076
  183.4 6.2 %copy-start.4 = (s32[128,2]{0,1:T(2,128)S(1)}, s32[128,2]{0,1:T(2,128)}, u32[]{:S(2)}) copy-start(s32[128,2]{0,1:T(2,128)} %param.11) | copy-start | bytes 3076
  183.4 54.7 %all-to-all-start.1 = ((bf16[3,8,48,896]{3,2,0,1:T(8,128)(2,1)}), bf16[3,8,48,896]{3,2,0,1:T(8,128)(2,1)}, u32[]{:S(2)}, u32[]{:S(2)}) async-start(bf16[3,8,48,896]{3,2,0,1:T(8,128)(2,1)} %copy.50), calls=%async_computation.1 | async-start | bytes 4128768 | tf_op jit(solution)/shard_map/all_to_all | solution.py:60
Sparse Core Ops, SparseCore 0:
  80.8 56.4 all-gather.2
